TPU v7x, 32 devices: a whole 2x2x4 slice. The times are simulated.
32 devices in a mesh: clip: 2 (over x), seq: 16 (over z, y, core).
Axes of the slice: x: 2, y: 2, z: 4, core: 2. Of those that a mesh axis runs over, the one named last changes fastest.
Arguments:
- video_query: bfloat16 [512, 4096], P(('clip', 'seq')), parts along dimension 0, may hold values from -6 to 6
- video_keys: bfloat16 [512, 4096], P(('clip', 'seq')), parts along dimension 0, may hold values from -6 to 6
- video_values: bfloat16 [512, 4096], P(('clip', 'seq')), parts along dimension 0, may hold values from -6 to 6
- audio_query: bfloat16 [256, 2048], P(('clip', 'seq')), parts along dimension 0, may hold values from -6 to 6
- audio_keys: bfloat16 [256, 2048], P(('clip', 'seq')), parts along dimension 0, may hold values from -6 to 6
- audio_values: bfloat16 [256, 2048], P(('clip', 'seq')), parts along dimension 0, may hold values from -6 to 6
- cross_video_query: bfloat16 [512, 2048], P(('clip', 'seq')), parts along dimension 0, may hold values from -6 to 6
- cross_video_keys: bfloat16 [512, 2048], P(('clip', 'seq')), parts along dimension 0, may hold values from -6 to 6
- cross_video_values: bfloat16 [512, 2048], P(('clip', 'seq')), parts along dimension 0, may hold values from -6 to 6
- cross_audio_query: bfloat16 [256, 2048], P(('clip', 'seq')), parts along dimension 0, may hold values from -6 to 6
- cross_audio_keys: bfloat16 [256, 2048], P(('clip', 'seq')), parts along dimension 0, may hold values from -6 to 6
- cross_audio_values: bfloat16 [256, 2048], P(('clip', 'seq')), parts along dimension 0, may hold values from -6 to 6
- video_length: int32 [2], P('clip'), parts along dimension 0, may hold values from 128 to 256
- audio_length: int32 [2], P('clip'), parts along dimension 0, may hold values from 64 to 128
- align_offset: int32 [2], P('clip'), parts along dimension 0, may hold values from -8 to 8
Outputs:
- video_mixed: bfloat16 [512, 4096], P(('clip', 'seq')), parts along dimension 0
- audio_mixed: bfloat16 [256, 2048], P(('clip', 'seq')), parts along dimension 0
- video_cross: bfloat16 [512, 2048], P(('clip', 'seq')), parts along dimension 0
- audio_cross: bfloat16 [256, 2048], P(('clip', 'seq')), parts along dimension 0
There are 2 independent parts, one for each index of `clip`. A program takes and returns all parts, laid end to end along the dimension named above; each array names one. Nothing has to cross between parts.
All inputs are finite; a program needn't handle non-finite values.
Results may differ from a plain program's by a relative error of at most 0.006.
Values may be sent and summed in bfloat16 or wider, within the bound.
A program may use at most 128 MiB of HBM per device.

v0:
```python
import functools
import math

import jax
import jax.numpy as jnp
from jax import lax
from jax.experimental import pallas as pl
from jax.experimental.pallas import tpu as pltpu
from jax.sharding import PartitionSpec as P

HV = 32
HDV = 128
HA = 32
HDA = 64


def block_size(total, limit):
    chosen = min(total, limit)
    while total % chosen:
        chosen -= 1
    return chosen


def split_heads(tokens, heads, depth, copies):
    rows = tokens.shape[0]
    shaped = tokens.reshape(copies, rows // copies, heads, depth).transpose(2, 0, 1, 3)
    return shaped.reshape(heads * copies, rows // copies, depth)


def spread_heads(tokens, heads, depth, copies):
    rows = tokens.shape[0]
    shaped = tokens.reshape(rows, heads, depth).transpose(1, 0, 2)
    shaped = jnp.broadcast_to(shaped[:, None], (heads, copies, rows, depth))
    return shaped.reshape(heads * copies, rows, depth)


def join_heads(owned, heads, depth, copies):
    part_rows = owned.shape[1]
    shaped = owned.reshape(heads, copies, part_rows, depth).transpose(1, 2, 0, 3)
    return shaped.reshape(copies * part_rows, heads * depth)


def owned_positions(rows, copies, devices, index):
    part_rows = rows // copies
    flat = jnp.arange(devices * part_rows, dtype=jnp.int32)
    return flat // part_rows * rows + index % copies * part_rows + flat % part_rows


def online_update(carry, scores, permit, value_tile, value_form):
    running, total, accum = carry
    scores = jnp.where(permit, scores, -1e30)
    newmax = jnp.maximum(running, jnp.max(scores, axis=2))
    weights = jnp.where(permit, jnp.exp(scores - newmax[:, :, None]), 0.0)
    factor = jnp.exp(running - newmax)
    total = total * factor + jnp.sum(weights, axis=2)
    mixed = jnp.einsum(
        value_form, weights.astype(jnp.bfloat16), value_tile, preferred_element_type=jnp.float32
    )
    accum = accum * factor[:, :, None] + mixed
    return (newmax, total, accum)


def fold_initial(rows, heads, depth):
    return (
        jnp.full((heads, rows), -1e30, jnp.float32),
        jnp.zeros((heads, rows), jnp.float32),
        jnp.zeros((heads, rows, depth), jnp.float32),
    )


def fold_piece(carry, local_query, key_rows, value_rows, permit, heads, depth):
    keyed = key_rows.reshape(key_rows.shape[0], heads, depth)
    valued = value_rows.reshape(value_rows.shape[0], heads, depth)
    scores = jnp.einsum("qhd,khd->hqk", local_query, keyed, preferred_element_type=jnp.float32) * (
        1.0 / math.sqrt(depth)
    )
    return online_update(carry, scores, permit[None], valued, "hqk,khd->hqd")


def fold_finish(carry, heads, depth):
    running, total, accum = carry
    result = (accum / total[:, :, None]).astype(jnp.bfloat16)
    return result.transpose(1, 0, 2).reshape(result.shape[1], heads * depth)


def attend_local(queries, keys, values, query_pos, key_pos, allowed):
    heads, q_count, depth = queries.shape
    k_count = keys.shape[1]
    q_block = block_size(q_count, 512)
    k_block = block_size(k_count, 2048)
    scale = 1.0 / math.sqrt(depth)
    q_tiles = queries.reshape(heads, q_count // q_block, q_block, depth).transpose(1, 0, 2, 3)
    k_tiles = keys.reshape(heads, k_count // k_block, k_block, depth).transpose(1, 0, 2, 3)
    v_tiles = values.reshape(heads, k_count // k_block, k_block, depth).transpose(1, 0, 2, 3)
    q_places = query_pos.reshape(q_count // q_block, q_block)
    k_places = key_pos.reshape(k_count // k_block, k_block)

    def one_tile(packed):
        q_tile, q_where = packed

        def absorb(carry, piece):
            k_tile, v_tile, k_where = piece
            scores = (
                jnp.einsum("hqd,hkd->hqk", q_tile, k_tile, preferred_element_type=jnp.float32)
                * scale
            )
            permit = allowed(q_where[:, None], k_where[None, :])[None]
            return (online_update(carry, scores, permit, v_tile, "hqk,hkd->hqd"), None)

        initial = fold_initial(q_block, heads, depth)
        final_state, unused = lax.scan(absorb, initial, (k_tiles, v_tiles, k_places))
        running, total, accum = final_state
        return (accum / total[:, :, None]).astype(jnp.bfloat16)

    tiles = lax.map(one_tile, (q_tiles, q_places))
    return tiles.transpose(1, 0, 2, 3).reshape(heads, q_count, depth)


def shards(
    video_query,
    video_keys,
    video_values,
    audio_query,
    audio_keys,
    audio_values,
    cross_video_query,
    cross_video_keys,
    cross_video_values,
    cross_audio_query,
    cross_audio_keys,
    cross_audio_values,
    video_length,
    audio_length,
    align_offset,
):
    devices = lax.axis_size("seq")
    index = lax.axis_index("seq")
    video_rows = video_query.shape[0]
    audio_rows = audio_query.shape[0]
    video_total = video_rows * devices
    audio_total = audio_rows * devices
    video_reach = video_total // 8
    audio_reach = 5 * audio_total // 8
    video_valid = video_length[0]
    audio_valid = audio_length[0]
    align_shift = align_offset[0]
    copies = max(devices // HV, 1)
    video_places = jnp.arange(video_total, dtype=jnp.int32)
    audio_places = jnp.arange(audio_total, dtype=jnp.int32)

    def video_open(q_where, k_where):
        return k_where < video_valid

    def toward_video(q_where, k_where):
        center = jnp.clip(q_where * audio_total // video_total + align_shift, 0, audio_valid - 1)
        return (k_where < audio_valid) & (jnp.abs(k_where - center) <= audio_reach)

    def toward_audio(q_where, k_where):
        center = jnp.clip((q_where - align_shift) * video_total // audio_total, 0, video_valid - 1)
        return (k_where < video_valid) & (jnp.abs(k_where - center) <= video_reach)

    video_owned = (
        lax.all_to_all(
            split_heads(video_query, HV, HDV, copies),
            "seq",
            split_axis=0,
            concat_axis=1,
            tiled=True,
        ),
        lax.all_to_all(
            spread_heads(video_keys, HV, HDV, copies),
            "seq",
            split_axis=0,
            concat_axis=1,
            tiled=True,
        ),
        lax.all_to_all(
            spread_heads(video_values, HV, HDV, copies),
            "seq",
            split_axis=0,
            concat_axis=1,
            tiled=True,
        ),
    )
    video_done = attend_local(
        video_owned[0],
        video_owned[1],
        video_owned[2],
        owned_positions(video_rows, copies, devices, index),
        video_places,
        video_open,
    )
    video_mixed = join_heads(
        lax.all_to_all(video_done, "seq", split_axis=1, concat_axis=0, tiled=True), HV, HDV, copies
    )
    audio_local = audio_query.reshape(audio_rows, HA, HDA)
    piece = (
        lax.all_gather(audio_keys, "seq", axis=0, tiled=True),
        lax.all_gather(audio_values, "seq", axis=0, tiled=True),
    )
    k_where = jnp.arange(piece[0].shape[0], dtype=jnp.int32)
    audio_k_where = k_where[None, :]
    permit = audio_k_where < audio_valid
    audio_state = fold_piece(
        fold_initial(audio_rows, HA, HDA), audio_local, piece[0], piece[1], permit, HA, HDA
    )
    audio_mixed = fold_finish(audio_state, HA, HDA)
    cross_owned = (
        lax.all_to_all(
            split_heads(cross_video_query, HA, HDA, copies),
            "seq",
            split_axis=0,
            concat_axis=1,
            tiled=True,
        ),
        lax.all_to_all(
            spread_heads(cross_audio_keys, HA, HDA, copies),
            "seq",
            split_axis=0,
            concat_axis=1,
            tiled=True,
        ),
        lax.all_to_all(
            spread_heads(cross_audio_values, HA, HDA, copies),
            "seq",
            split_axis=0,
            concat_axis=1,
            tiled=True,
        ),
    )
    cross_done = attend_local(
        cross_owned[0],
        cross_owned[1],
        cross_owned[2],
        owned_positions(video_rows, copies, devices, index),
        audio_places,
        toward_video,
    )
    video_cross = join_heads(
        lax.all_to_all(cross_done, "seq", split_axis=1, concat_axis=0, tiled=True), HA, HDA, copies
    )
    listen_owned = (
        lax.all_to_all(
            split_heads(cross_audio_query, HA, HDA, copies),
            "seq",
            split_axis=0,
            concat_axis=1,
            tiled=True,
        ),
        lax.all_to_all(
            spread_heads(cross_video_keys, HA, HDA, copies),
            "seq",
            split_axis=0,
            concat_axis=1,
            tiled=True,
        ),
        lax.all_to_all(
            spread_heads(cross_video_values, HA, HDA, copies),
            "seq",
            split_axis=0,
            concat_axis=1,
            tiled=True,
        ),
    )
    listen_done = attend_local(
        listen_owned[0],
        listen_owned[1],
        listen_owned[2],
        owned_positions(audio_rows, copies, devices, index),
        video_places,
        toward_audio,
    )
    audio_cross = join_heads(
        lax.all_to_all(listen_done, "seq", split_axis=1, concat_axis=0, tiled=True), HA, HDA, copies
    )
    return (video_mixed, audio_mixed, video_cross, audio_cross)


LANES = 128

GROUPS = (
    ((0, 1, 2), 0, False),
    ((3, 4, 5), 1, False),
    ((6, 10, 11), 2, True),
    ((9, 7, 8), 3, True),
)


def softmax_mix(query, keys, values, permit, scale):
    scores = lax.dot_general(
        query, keys, (((1,), (1,)), ((), ())), preferred_element_type=jnp.float32
    )
    scores = jnp.where(permit, scores * scale, -1e30)
    peak = jnp.max(scores, axis=1, keepdims=True)
    weights = jnp.exp(scores - peak)
    total = jnp.sum(weights, axis=1, keepdims=True)
    mixed = jnp.dot(weights.astype(jnp.bfloat16), values, preferred_element_type=jnp.float32)
    return mixed / total


def read_tokens(ref, column):
    block = ref[:, :, column : column + LANES]
    n, rows, _ = block.shape
    if rows % 16:
        return block.astype(jnp.float32).reshape(n * rows, LANES).astype(block.dtype)
    return block.reshape(n * rows, LANES)


def write_tokens(ref, column, result):
    n, rows, _ = ref.shape
    ref[:, :, column : column + LANES] = result.reshape(n, rows, LANES).astype(ref.dtype)


def margin_blocks(n, video_rows):
    return min(-(-(3 * n * video_rows // 16) // video_rows), n // 2)


def held_shapes(n, arrays):
    half = n // 2
    shapes = [None] * 12
    for group, which, halved in GROUPS:
        for place, at in enumerate(group):
            rows, cols = arrays[at].shape
            blocks = n
            if halved and place == 0:
                blocks = half
            elif which == 3:
                blocks = half + margin_blocks(n, rows)
            shapes[at] = (blocks, rows, cols // (half if halved else n))
    return shapes


def fused_kernel(n, ratio, *refs):
    video_length, audio_length, align_offset = refs[:3]
    arrays = refs[3:15]
    outs = refs[15:19]
    held = refs[19:31]
    results = refs[31:35]
    send_sem, far_sem, recv_sem, back_send, back_recv = refs[35:]
    half = n // 2
    margin = held[7].shape[0] - half
    me = lax.axis_index("seq")
    side = me // half
    inner = lax.rem(me, half)
    near = (me >= half - margin) & (me < half + margin)

    def columns(width, owner):
        return pl.ds(pl.multiple_of(owner * width, LANES), width)

    def slot_of(group, which, halved, at, to_side):
        if halved and at == group[0]:
            return inner
        if which == 3:
            return me - to_side * (half - margin)
        return me

    def send(at, owner, slot, peer, sem):
        pltpu.make_async_remote_copy(
            src_ref=arrays[at].at[:, columns(held[at].shape[2], owner)],
            dst_ref=held[at].at[slot],
            send_sem=sem.at[at],
            recv_sem=recv_sem.at[at],
            device_id={"seq": peer},
            device_id_type=pl.DeviceIdType.MESH,
        ).start()

    for group, which, halved in GROUPS:
        for at in group:
            pltpu.make_async_copy(
                arrays[at].at[:, columns(held[at].shape[2], inner if halved else me)],
                held[at].at[slot_of(group, which, halved, at, side)],
                recv_sem.at[at],
            ).start()

    barrier = pltpu.get_barrier_semaphore()

    @pl.loop(1, n)
    def _(step):
        pl.semaphore_signal(
            barrier,
            inc=1,
            device_id={"seq": lax.rem(me + step, n)},
            device_id_type=pl.DeviceIdType.MESH,
        )

    pl.semaphore_wait(barrier, n - 1)

    for group, which, halved in GROUPS:
        if not halved:

            @pl.loop(0, half)
            def _(step, group=group):
                peer = (1 - side) * half + lax.rem(inner + step, half)
                for at in group:
                    send(at, peer, me, peer, far_sem)

            @pl.loop(1, half)
            def _(step, group=group):
                peer = side * half + lax.rem(inner + step, half)
                for at in group:
                    send(at, peer, me, peer, send_sem)

            continue

        def far_sends(group=group, which=which):
            @pl.loop(0, half)
            def _(step):
                owner = lax.rem(inner + step, half)
                for at in group[1:]:
                    slot = slot_of(group, which, True, at, 1 - side)
                    send(at, owner, slot, (1 - side) * half + owner, far_sem)

        if which == 3:
            pl.when(near)(far_sends)
        else:
            far_sends()

        @pl.loop(1, half)
        def _(step, group=group, which=which):
            owner = lax.rem(inner + step, half)
            for at in group:
                slot = slot_of(group, which, True, at, side)
                send(at, owner, slot, side * half + owner, send_sem)

    video_valid = video_length[0]
    audio_valid = audio_length[0]
    shift = align_offset[0]
    video_rows = arrays[0].shape[0]
    audio_rows = arrays[3].shape[0]
    video_total = n * video_rows
    audio_total = n * audio_rows
    video_reach = video_total // 8
    audio_reach = 5 * audio_total // 8

    def query_places(count, copies, first):
        rows = first + lax.broadcasted_iota(jnp.int32, (count, 1), 0)
        return jnp.concatenate([rows] * copies, axis=0)

    def key_places(count):
        return lax.broadcasted_iota(jnp.int32, (1, count), 1)

    def permit_of(which, copies):
        if which == 0:
            return key_places(video_total) < video_valid
        if which == 1:
            return key_places(audio_total) < audio_valid
        if which == 2:
            where = key_places(audio_total)
            spots = query_places(half * video_rows, copies, side * half * video_rows)
            spots = lax.shift_right_logical(spots, ratio.bit_length() - 1)
            center = jnp.clip(spots + shift, 0, audio_valid - 1)
            return (where < audio_valid) & (jnp.abs(where - center) <= audio_reach)
        where = key_places((half + margin) * video_rows) + side * (half - margin) * video_rows
        spots = query_places(half * audio_rows, copies, side * half * audio_rows)
        center = jnp.clip((spots - shift) * ratio, 0, video_valid - 1)
        return (where < video_valid) & (jnp.abs(where - center) <= video_reach)

    for group, which, halved in GROUPS:
        for at in group:
            pltpu.make_async_copy(held[at], held[at], recv_sem.at[at]).wait()
        query, keys, values = (held[at] for at in group)
        depth = HDV if which == 0 else HDA
        copies = LANES // depth
        scale = 1.0 / math.sqrt(depth)
        permit = permit_of(which, copies)
        for column in range(0, query.shape[2], LANES):
            tokens = read_tokens(query, column)
            if copies > 1:
                lane = lax.broadcasted_iota(jnp.int32, tokens.shape, 1) // depth
                zero = jnp.zeros_like(tokens)
                tokens = jnp.concatenate(
                    [jnp.where(lane == head, tokens, zero) for head in range(copies)], axis=0
                )
            mixed = softmax_mix(
                tokens, read_tokens(keys, column), read_tokens(values, column), permit, scale
            )
            if copies > 1:
                rows = mixed.shape[0] // copies
                merged = mixed[:rows]
                lane = lax.broadcasted_iota(jnp.int32, merged.shape, 1) // depth
                for head in range(1, copies):
                    merged = jnp.where(lane == head, mixed[head * rows : (head + 1) * rows], merged)
                mixed = merged
            write_tokens(results[which], column, mixed)
        mine = inner if halved else me
        count = half if halved else n
        first = side * half if halved else 0
        target = outs[which].at[:, columns(results[which].shape[2], mine)]
        pltpu.make_async_copy(results[which].at[mine], target, back_recv.at[which]).start()

        @pl.loop(1, count)
        def _(step, which=which, target=target, mine=mine, count=count, first=first):
            block = lax.rem(mine + step, count)
            pltpu.make_async_remote_copy(
                src_ref=results[which].at[block],
                dst_ref=target,
                send_sem=back_send.at[which],
                recv_sem=back_recv.at[which],
                device_id={"seq": first + block},
                device_id_type=pl.DeviceIdType.MESH,
            ).start()

    def wait_bytes(ref, blocks, sem):
        part = ref.at[pl.ds(0, blocks)]
        pltpu.make_async_copy(part, part, sem).wait()

    for group, which, halved in GROUPS:
        for at in group:
            wait_bytes(held[at], half - 1, send_sem.at[at])
            if not halved or (which == 2 and at != group[0]):
                wait_bytes(held[at], half, far_sem.at[at])
            elif at != group[0]:

                @pl.when(near)
                def _(at=at):
                    wait_bytes(held[at], half, far_sem.at[at])

    for which in range(4):
        wait_bytes(results[which], results[which].shape[0] - 1, back_send.at[which])
        pltpu.make_async_copy(outs[which], outs[which], back_recv.at[which]).wait()


def write_out(*refs):
    sources, targets, sem = refs[:4], refs[4:8], refs[8]
    copies = [pltpu.make_async_copy(*pair, sem.at[at]) for at, pair in enumerate(zip(sources, targets))]
    for copy in copies:
        copy.start()
    for copy in copies:
        copy.wait()


def fused_shards(*arguments):
    n = lax.axis_size("seq")
    arrays = arguments[:12]
    lengths = arguments[12:]
    arrays = [pltpu.with_memory_space_constraint(a, pltpu.HBM) for a in arrays]
    ratio = arrays[0].shape[0] // arrays[3].shape[0]
    held = [pltpu.VMEM(s, a.dtype) for s, a in zip(held_shapes(n, arrays), arrays)]
    results = [
        pltpu.VMEM((n, *held[0].shape[1:]), jnp.bfloat16),
        pltpu.VMEM((n, *held[3].shape[1:]), jnp.bfloat16),
        pltpu.VMEM((n // 2, *held[6].shape[1:]), jnp.bfloat16),
        pltpu.VMEM((n // 2, *held[9].shape[1:]), jnp.bfloat16),
    ]
    shapes = [arrays[at].shape for at in (0, 3, 6, 9)]
    anywhere = pl.BlockSpec(memory_space=pl.ANY)
    scalars = pl.BlockSpec(memory_space=pltpu.SMEM)
    vectors = pl.BlockSpec(memory_space=pltpu.VMEM)
    mixed = pl.pallas_call(
        functools.partial(fused_kernel, n, ratio),
        out_shape=tuple(pltpu.VMEM(shape, jnp.bfloat16) for shape in shapes),
        in_specs=[scalars] * 3 + [pl.BlockSpec(memory_space=pltpu.HBM)] * 12,
        out_specs=(vectors,) * 4,
        scratch_shapes=held
        + results
        + [
            pltpu.SemaphoreType.DMA((12,)),
            pltpu.SemaphoreType.DMA((12,)),
            pltpu.SemaphoreType.DMA((12,)),
            pltpu.SemaphoreType.DMA((4,)),
            pltpu.SemaphoreType.DMA((4,)),
        ],
        compiler_params=pltpu.CompilerParams(
            collective_id=0, has_side_effects=True, vmem_limit_bytes=24 * 2**20
        ),
    )(*lengths, *arrays)
    return pl.pallas_call(
        write_out,
        out_shape=tuple(jax.ShapeDtypeStruct(shape, jnp.bfloat16) for shape in shapes),
        in_specs=[vectors] * 4,
        out_specs=(anywhere,) * 4,
        scratch_shapes=[pltpu.SemaphoreType.DMA((4,))],
        compiler_params=pltpu.CompilerParams(vmem_limit_bytes=2**20),
    )(*mixed)


def kernel_fits(n, video_rows, audio_rows):
    if n < 4 or n % 2 or HV % n or HA % n or (HV // n * HDV) % LANES or (HA // n * HDA) % LANES:
        return False
    ratio = video_rows // audio_rows
    return video_rows == ratio * audio_rows and ratio & (ratio - 1) == 0 and n * audio_rows % 16 == 0 and audio_rows % 8 == 0


def dispatch(*arguments):
    fits = kernel_fits(lax.axis_size("seq"), arguments[0].shape[0], arguments[3].shape[0])
    return (fused_shards if fits else shards)(*arguments)


def solution(mesh):
    placed = (
        P(("clip", "seq"), None),
        P(("clip", "seq"), None),
        P(("clip", "seq"), None),
        P(("clip", "seq"), None),
        P(("clip", "seq"), None),
        P(("clip", "seq"), None),
        P(("clip", "seq"), None),
        P(("clip", "seq"), None),
        P(("clip", "seq"), None),
        P(("clip", "seq"), None),
        P(("clip", "seq"), None),
        P(("clip", "seq"), None),
        P("clip"),
        P("clip"),
        P("clip"),
    )
    return jax.shard_map(
        dispatch,
        mesh=mesh,
        in_specs=placed,
        out_specs=(
            P(("clip", "seq"), None),
            P(("clip", "seq"), None),
            P(("clip", "seq"), None),
            P(("clip", "seq"), None),
        ),
        check_vma=False,
    )
```

profile of v0, /device:TPU:0, one launch (start us, length us, event | category | flops | bytes accessed | tf_op | source)
XLA Modules:
  0.0 32.9 jit_solution(12218664567584494750)
XLA Ops:
  2.6 29.6 %shard_map.174 = (bf16[16,4096]{1,0:T(8,128)(2,1)S(1)}, bf16[8,2048]{1,0:T(8,128)(2,1)S(1)}, bf16[16,2048]{1,0:T(8,128)(2,1)S(1)}, bf16[8,2048]{1,0:T(8,128)(2,1)S(1)}) custom-call(s32[1]{0:T(128)S(6)} %copy.19.refs_0_, s32[1]{0:T(128)S(6)} %copy.20.refs_1_, s32[1]{0:T(128)S(6)} %copy.21.refs_2_, bf16[16,4096]{1,0:T(8,128)(2,1)} %refs_3_.1, ...), custom_call_target="tpu_custom_call" | custom-call | tf_op jit(solution)/shard_map/pallas_call | solution.py:549
  32.2 0.7 %shard_map.175 = (bf16[16,4096]{1,0:T(8,128)(2,1)}, bf16[8,2048]{1,0:T(8,128)(2,1)}, bf16[16,2048]{1,0:T(8,128)(2,1)}, bf16[8,2048]{1,0:T(8,128)(2,1)}) custom-call(bf16[16,4096]{1,0:T(8,128)(2,1)S(1)} %get-tuple-element.8.refs_0_, bf16[8,2048]{1,0:T(8,128)(2,1)S(1)} %get-tuple-element.9.refs_1_, bf16[16,2048]{1,0:T(8,128)(2,1)S(1)} %get-tuple-element.10.refs_2_, ...), custom_call_target="tpu_custom_call" | custom-call | tf_op jit(solution)/shard_map/pallas_call | solution.py:567
where the time goes:
time: 33.1 us; the launch traced here: 32.9 us
  Pallas kernels  30.3 us (92%)
  between operations  2.58 us (8%)
    pallas_call x1, Pallas kernels, fused_shards(): pl.pallas_call(functools.partial(fused_kernel, n, ratio), out_shape=tuple...  29.6 us
    pallas_call x1, Pallas kernels, fused_shards(): pl.pallas_call(write_out, out_shape=tuple((jax.ShapeDtypeStruct(shape, jn...  0.73 us

commit v1 on v0

--- a/solution.py
+++ b/solution.py
@@ -336,8 +336,9 @@
     outs = refs[15:19]
     held = refs[19:31]
     results = refs[31:35]
-    send_sem, far_sem, recv_sem, back_send, back_recv = refs[35:]
+    send_sem, far_sem, recv_sem, back_send, back_recv, stage_sem = refs[35:]
     half = n // 2
+    quarter = n // 4
     margin = held[7].shape[0] - half
     me = lax.axis_index("seq")
     side = me // half
@@ -372,55 +373,92 @@
                 recv_sem.at[at],
             ).start()
 
+    level = me // quarter
+    rank = lax.rem(me, quarter)
+    central = (level == 1) | (level == 2)
+    here = level * quarter
+    sibling = (level + 1 - 2 * lax.rem(level, 2)) * quarter
+    far_center = (2 - side) * quarter
+    far_edge = (3 - 3 * side) * quarter
+
     barrier = pltpu.get_barrier_semaphore()
 
-    @pl.loop(1, n)
+    def signal(sem, peer):
+        pl.semaphore_signal(
+            sem, inc=1, device_id={"seq": peer}, device_id_type=pl.DeviceIdType.MESH
+        )
+
+    @pl.loop(1, quarter)
     def _(step):
-        pl.semaphore_signal(
-            barrier,
-            inc=1,
-            device_id={"seq": lax.rem(me + step, n)},
-            device_id_type=pl.DeviceIdType.MESH,
-        )
-
-    pl.semaphore_wait(barrier, n - 1)
-
-    for group, which, halved in GROUPS:
-        if not halved:
-
-            @pl.loop(0, half)
-            def _(step, group=group):
-                peer = (1 - side) * half + lax.rem(inner + step, half)
+        signal(barrier, here + lax.rem(rank + step, quarter))
+
+    @pl.loop(0, quarter)
+    def _(step):
+        signal(barrier, sibling + lax.rem(rank + step, quarter))
+
+    @pl.when(central)
+    def _():
+        @pl.loop(0, quarter)
+        def _(step):
+            signal(barrier, far_center + lax.rem(rank + step, quarter))
+
+    pl.semaphore_wait(barrier, jnp.where(central, 3 * quarter - 1, 2 * quarter - 1))
+
+    def send_level(number, base, first, same):
+        group, which, halved = GROUPS[number]
+
+        def sends():
+            @pl.loop(first, quarter)
+            def _(step):
+                peer = base + lax.rem(rank + step, quarter)
+                owner = lax.rem(peer, half) if halved else peer
                 for at in group:
-                    send(at, peer, me, peer, far_sem)
-
-            @pl.loop(1, half)
-            def _(step, group=group):
-                peer = side * half + lax.rem(inner + step, half)
-                for at in group:
-                    send(at, peer, me, peer, send_sem)
-
-            continue
-
-        def far_sends(group=group, which=which):
-            @pl.loop(0, half)
-            def _(step):
-                owner = lax.rem(inner + step, half)
-                for at in group[1:]:
-                    slot = slot_of(group, which, True, at, 1 - side)
-                    send(at, owner, slot, (1 - side) * half + owner, far_sem)
-
-        if which == 3:
-            pl.when(near)(far_sends)
+                    if halved and at == group[0] and not same:
+                        continue
+                    slot = slot_of(group, which, halved, at, side if same else 1 - side)
+                    send(at, owner, slot, peer, send_sem if same else far_sem)
+
+        if which == 3 and not same:
+            pl.when(near)(sends)
         else:
-            far_sends()
-
-        @pl.loop(1, half)
-        def _(step, group=group, which=which):
-            owner = lax.rem(inner + step, half)
-            for at in group:
-                slot = slot_of(group, which, True, at, side)
-                send(at, owner, slot, side * half + owner, send_sem)
+            sends()
+
+    order = (0, 1, 2, 3)
+    lead = order[0]
+
+    @pl.when(central)
+    def _():
+        signal(stage_sem.at[0], sibling + rank)
+        signal(stage_sem.at[1], far_center + rank)
+        send_level(lead, far_center, 0, False)
+
+    send_level(lead, sibling, 0, True)
+    send_level(lead, here, 1, True)
+
+    @pl.when(central)
+    def _():
+        pl.semaphore_wait(stage_sem.at[1], 1)
+        signal(stage_sem.at[2], sibling + rank)
+
+    @pl.when(jnp.logical_not(central))
+    def _():
+        pl.semaphore_wait(stage_sem.at[0], 1)
+        send_level(lead, far_center, 0, False)
+        pl.semaphore_wait(stage_sem.at[2], 1)
+
+    send_level(lead, far_edge, 0, False)
+    send_level(1, far_center, 0, False)
+    send_level(1, far_edge, 0, False)
+    send_level(2, far_center, 0, False)
+    send_level(2, far_edge, 0, False)
+    send_level(3, far_center, 0, False)
+    send_level(3, far_edge, 0, False)
+    send_level(1, sibling, 0, True)
+    send_level(1, here, 1, True)
+    send_level(2, sibling, 0, True)
+    send_level(2, here, 1, True)
+    send_level(3, sibling, 0, True)
+    send_level(3, here, 1, True)
 
     video_valid = video_length[0]
     audio_valid = audio_length[0]
@@ -455,7 +493,8 @@
         center = jnp.clip((spots - shift) * ratio, 0, video_valid - 1)
         return (where < video_valid) & (jnp.abs(where - center) <= video_reach)
 
-    for group, which, halved in GROUPS:
+    def compute(number):
+        group, which, halved = GROUPS[number]
         for at in group:
             pltpu.make_async_copy(held[at], held[at], recv_sem.at[at]).wait()
         query, keys, values = (held[at] for at in group)
@@ -482,23 +521,48 @@
                     merged = jnp.where(lane == head, mixed[head * rows : (head + 1) * rows], merged)
                 mixed = merged
             write_tokens(results[which], column, mixed)
+
+    def give_back(number):
+        group, which, halved = GROUPS[number]
         mine = inner if halved else me
-        count = half if halved else n
-        first = side * half if halved else 0
         target = outs[which].at[:, columns(results[which].shape[2], mine)]
-        pltpu.make_async_copy(results[which].at[mine], target, back_recv.at[which]).start()
-
-        @pl.loop(1, count)
-        def _(step, which=which, target=target, mine=mine, count=count, first=first):
-            block = lax.rem(mine + step, count)
+
+        def give(block, peer):
             pltpu.make_async_remote_copy(
                 src_ref=results[which].at[block],
                 dst_ref=target,
                 send_sem=back_send.at[which],
                 recv_sem=back_recv.at[which],
-                device_id={"seq": first + block},
+                device_id={"seq": peer},
                 device_id_type=pl.DeviceIdType.MESH,
             ).start()
+
+        if not halved:
+
+            @pl.loop(0, half)
+            def _(step):
+                peer = (1 - side) * half + step
+                give(peer, peer)
+
+        @pl.loop(1, half)
+        def _(step):
+            block = lax.rem(inner + step, half)
+            peer = side * half + block
+            give(block if halved else peer, peer)
+
+        pltpu.make_async_copy(results[which].at[mine], target, back_recv.at[which]).start()
+
+    compute(0)
+    compute(1)
+    compute(2)
+    give_back(2)
+    give_back(0)
+    give_back(1)
+    compute(3)
+    give_back(3)
+
+    for which in range(4):
+        pltpu.make_async_copy(outs[which], outs[which], back_recv.at[which]).wait()
 
     def wait_bytes(ref, blocks, sem):
         part = ref.at[pl.ds(0, blocks)]
@@ -517,7 +581,6 @@
 
     for which in range(4):
         wait_bytes(results[which], results[which].shape[0] - 1, back_send.at[which])
-        pltpu.make_async_copy(outs[which], outs[which], back_recv.at[which]).wait()
 
 
 def write_out(*refs):
@@ -559,6 +622,7 @@
             pltpu.SemaphoreType.DMA((12,)),
             pltpu.SemaphoreType.DMA((4,)),
             pltpu.SemaphoreType.DMA((4,)),
+            pltpu.SemaphoreType.REGULAR((3,)),
         ],
         compiler_params=pltpu.CompilerParams(
             collective_id=0, has_side_effects=True, vmem_limit_bytes=24 * 2**20
@@ -575,7 +639,7 @@
 
 
 def kernel_fits(n, video_rows, audio_rows):
-    if n < 4 or n % 2 or HV % n or HA % n or (HV // n * HDV) % LANES or (HA // n * HDA) % LANES:
+    if n < 4 or n % 4 or HV % n or HA % n or (HV // n * HDV) % LANES or (HA // n * HDA) % LANES:
         return False
     ratio = video_rows // audio_rows
     return video_rows == ratio * audio_rows and ratio & (ratio - 1) == 0 and n * audio_rows % 16 == 0 and audio_rows % 8 == 0

time: 33.1 us -> 32.6 us (0.985)
  Pallas kernels: 30.3 us -> 29.9 us
    pallas_call x1, Pallas kernels: 29.6 us -> 29.2 us  [fused_shards(): pl.pallas_call(functools.partial(fused_kernel, n, ratio), out_shape=tuple...]
where the time goes in v1:
time: 32.6 us; the launch traced here: 32.5 us
  Pallas kernels  29.9 us (92%)
  between operations  2.58 us (8%)
    pallas_call x1, Pallas kernels, fused_shards(): pl.pallas_call(functools.partial(fused_kernel, n, ratio), out_shape=tuple...  29.2 us
    pallas_call x1, Pallas kernels, fused_shards(): pl.pallas_call(write_out, out_shape=tuple((jax.ShapeDtypeStruct(shape, jn...  0.73 us

profile of v1, /device:TPU:0, one launch (start us, length us, event | category | flops | bytes accessed | tf_op | source)
XLA Modules:
  0.0 32.5 jit_solution(1275933257057778326)
XLA Ops:
  2.6 29.2 %shard_map.174 = (bf16[16,4096]{1,0:T(8,128)(2,1)S(1)}, bf16[8,2048]{1,0:T(8,128)(2,1)S(1)}, bf16[16,2048]{1,0:T(8,128)(2,1)S(1)}, bf16[8,2048]{1,0:T(8,128)(2,1)S(1)}) custom-call(s32[1]{0:T(128)S(6)} %copy.19.refs_0_, s32[1]{0:T(128)S(6)} %copy.20.refs_1_, s32[1]{0:T(128)S(6)} %copy.21.refs_2_, bf16[16,4096]{1,0:T(8,128)(2,1)} %refs_3_.1, ...), custom_call_target="tpu_custom_call" | custom-call | tf_op jit(solution)/shard_map/pallas_call | solution.py:612
  31.7 0.7 %shard_map.175 = (bf16[16,4096]{1,0:T(8,128)(2,1)}, bf16[8,2048]{1,0:T(8,128)(2,1)}, bf16[16,2048]{1,0:T(8,128)(2,1)}, bf16[8,2048]{1,0:T(8,128)(2,1)}) custom-call(bf16[16,4096]{1,0:T(8,128)(2,1)S(1)} %get-tuple-element.8.refs_0_, bf16[8,2048]{1,0:T(8,128)(2,1)S(1)} %get-tuple-element.9.refs_1_, bf16[16,2048]{1,0:T(8,128)(2,1)S(1)} %get-tuple-element.10.refs_2_, ...), custom_call_target="tpu_custom_call" | custom-call | tf_op jit(solution)/shard_map/pallas_call | solution.py:631

commit v2 on v1

--- a/solution.py
+++ b/solution.py
@@ -1,3 +1,4 @@
+import contextlib
 import functools
 import math
 
@@ -277,6 +278,7 @@
 
 
 LANES = 128
+mark = lambda name: contextlib.nullcontext()
 
 GROUPS = (
     ((0, 1, 2), 0, False),
@@ -373,8 +375,12 @@
                 recv_sem.at[at],
             ).start()
 
+    col = quarter // 2
     level = me // quarter
     rank = lax.rem(me, quarter)
+    core = lax.rem(rank, col)
+    mine_col = rank - core
+    next_col = col - mine_col
     central = (level == 1) | (level == 2)
     here = level * quarter
     sibling = (level + 1 - 2 * lax.rem(level, 2)) * quarter
@@ -388,29 +394,33 @@
             sem, inc=1, device_id={"seq": peer}, device_id_type=pl.DeviceIdType.MESH
         )
 
-    @pl.loop(1, quarter)
-    def _(step):
-        signal(barrier, here + lax.rem(rank + step, quarter))
-
-    @pl.loop(0, quarter)
-    def _(step):
-        signal(barrier, sibling + lax.rem(rank + step, quarter))
+    def greet(base, first):
+        @pl.loop(first, col)
+        def _(step):
+            signal(barrier, base + lax.rem(core + step, col))
 
     @pl.when(central)
     def _():
-        @pl.loop(0, quarter)
-        def _(step):
-            signal(barrier, far_center + lax.rem(rank + step, quarter))
-
-    pl.semaphore_wait(barrier, jnp.where(central, 3 * quarter - 1, 2 * quarter - 1))
-
-    def send_level(number, base, first, same):
+        greet(far_center + mine_col, 0)
+
+    greet(here + mine_col, 1)
+
+    @pl.when(central)
+    def _():
+        greet(here + next_col, 0)
+        greet(sibling + mine_col, 0)
+
+    with mark("BAR"):
+        pl.semaphore_wait(barrier, jnp.where(central, 3 * col - 1, 2 * col - 1))
+
+    def send_part(number, base, count, first, same):
         group, which, halved = GROUPS[number]
+        spot = core if count == col else rank
 
         def sends():
-            @pl.loop(first, quarter)
+            @pl.loop(first, count)
             def _(step):
-                peer = base + lax.rem(rank + step, quarter)
+                peer = base + lax.rem(spot + step, count)
                 owner = lax.rem(peer, half) if halved else peer
                 for at in group:
                     if halved and at == group[0] and not same:
@@ -423,42 +433,69 @@
         else:
             sends()
 
-    order = (0, 1, 2, 3)
-    lead = order[0]
+    def f(number):
+        send_part(number, far_edge, quarter, 0, False)
+        send_part(number, far_center, quarter, 0, False)
+
+    def s(number):
+        send_part(number, sibling, quarter, 0, True)
+
+    def h(number):
+        send_part(number, here, quarter, 1, True)
+
+    across = rank + next_col - mine_col
 
     @pl.when(central)
     def _():
-        signal(stage_sem.at[0], sibling + rank)
-        signal(stage_sem.at[1], far_center + rank)
-        send_level(lead, far_center, 0, False)
-
-    send_level(lead, sibling, 0, True)
-    send_level(lead, here, 1, True)
-
-    @pl.when(central)
-    def _():
-        pl.semaphore_wait(stage_sem.at[1], 1)
-        signal(stage_sem.at[2], sibling + rank)
+        signal(stage_sem.at[0], here + across)
+        send_part(0, far_center + mine_col, col, 0, False)
+        h(0)
+        with mark("Y"):
+            pl.semaphore_wait(stage_sem.at[0], 1)
+        send_part(0, far_center + next_col, col, 0, False)
+        with mark("O"):
+            pl.semaphore_wait(stage_sem.at[2], 1)
+        signal(stage_sem.at[1], sibling + rank)
+        signal(stage_sem.at[5], here + across)
+        with mark("Y2"):
+            pl.semaphore_wait(stage_sem.at[5], 1)
+        signal(stage_sem.at[3], far_center + rank)
+        s(0)
+        with mark("B"):
+            pl.semaphore_wait(stage_sem.at[3], 1)
+        signal(stage_sem.at[4], sibling + rank)
+        send_part(0, far_edge, quarter, 0, False)
+        f(1)
+        f(3)
+        f(2)
+        h(1)
+        s(1)
+        h(3)
+        s(3)
+        h(2)
+        s(2)
 
     @pl.when(jnp.logical_not(central))
     def _():
-        pl.semaphore_wait(stage_sem.at[0], 1)
-        send_level(lead, far_center, 0, False)
-        pl.semaphore_wait(stage_sem.at[2], 1)
-
-    send_level(lead, far_edge, 0, False)
-    send_level(1, far_center, 0, False)
-    send_level(1, far_edge, 0, False)
-    send_level(2, far_center, 0, False)
-    send_level(2, far_edge, 0, False)
-    send_level(3, far_center, 0, False)
-    send_level(3, far_edge, 0, False)
-    send_level(1, sibling, 0, True)
-    send_level(1, here, 1, True)
-    send_level(2, sibling, 0, True)
-    send_level(2, here, 1, True)
-    send_level(3, sibling, 0, True)
-    send_level(3, here, 1, True)
+        signal(stage_sem.at[2], sibling + rank)
+        send_part(0, sibling + mine_col, col, 0, True)
+        send_part(0, here + mine_col, col, 1, True)
+        with mark("A"):
+            pl.semaphore_wait(stage_sem.at[1], 1)
+        send_part(0, sibling + next_col, col, 0, True)
+        send_part(0, far_center, quarter, 0, False)
+        with mark("C"):
+            pl.semaphore_wait(stage_sem.at[4], 1)
+        send_part(0, far_edge, quarter, 0, False)
+        send_part(0, here + next_col, col, 0, True)
+        f(1)
+        s(1)
+        s(3)
+        f(2)
+        s(2)
+        h(1)
+        h(3)
+        h(2)
 
     video_valid = video_length[0]
     audio_valid = audio_length[0]
@@ -496,7 +533,8 @@
     def compute(number):
         group, which, halved = GROUPS[number]
         for at in group:
-            pltpu.make_async_copy(held[at], held[at], recv_sem.at[at]).wait()
+            with mark("W%d_%d" % (which, at)):
+                pltpu.make_async_copy(held[at], held[at], recv_sem.at[at]).wait()
         query, keys, values = (held[at] for at in group)
         depth = HDV if which == 0 else HDA
         copies = LANES // depth
@@ -522,7 +560,7 @@
                 mixed = merged
             write_tokens(results[which], column, mixed)
 
-    def give_back(number):
+    def give_back(number, far=False, close=False):
         group, which, halved = GROUPS[number]
         mine = inner if halved else me
         target = outs[which].at[:, columns(results[which].shape[2], mine)]
@@ -537,12 +575,15 @@
                 device_id_type=pl.DeviceIdType.MESH,
             ).start()
 
-        if not halved:
+        if far:
 
             @pl.loop(0, half)
             def _(step):
                 peer = (1 - side) * half + step
                 give(peer, peer)
+
+        if not close:
+            return
 
         @pl.loop(1, half)
         def _(step):
@@ -553,16 +594,21 @@
         pltpu.make_async_copy(results[which].at[mine], target, back_recv.at[which]).start()
 
     compute(0)
+    give_back(0, close=True)
+    pl.when(central)(lambda: give_back(0, far=True))
     compute(1)
+    give_back(1, close=True)
+    pl.when(central)(lambda: give_back(1, far=True))
+    compute(3)
+    give_back(3, far=False, close=True)
+    pl.when(jnp.logical_not(central))(lambda: give_back(0, far=True))
+    pl.when(jnp.logical_not(central))(lambda: give_back(1, far=True))
     compute(2)
-    give_back(2)
-    give_back(0)
-    give_back(1)
-    compute(3)
-    give_back(3)
+    give_back(2, far=False, close=True)
 
     for which in range(4):
-        pltpu.make_async_copy(outs[which], outs[which], back_recv.at[which]).wait()
+        with mark("R%d" % which):
+            pltpu.make_async_copy(outs[which], outs[which], back_recv.at[which]).wait()
 
     def wait_bytes(ref, blocks, sem):
         part = ref.at[pl.ds(0, blocks)]
@@ -622,7 +668,7 @@
             pltpu.SemaphoreType.DMA((12,)),
             pltpu.SemaphoreType.DMA((4,)),
             pltpu.SemaphoreType.DMA((4,)),
-            pltpu.SemaphoreType.REGULAR((3,)),
+            pltpu.SemaphoreType.REGULAR((6,)),
         ],
         compiler_params=pltpu.CompilerParams(
             collective_id=0, has_side_effects=True, vmem_limit_bytes=24 * 2**20
@@ -639,7 +685,7 @@
 
 
 def kernel_fits(n, video_rows, audio_rows):
-    if n < 4 or n % 4 or HV % n or HA % n or (HV // n * HDV) % LANES or (HA // n * HDA) % LANES:
+    if n % 16 or HV % n or HA % n or (HV // n * HDV) % LANES or (HA // n * HDA) % LANES:
         return False
     ratio = video_rows // audio_rows
     return video_rows == ratio * audio_rows and ratio & (ratio - 1) == 0 and n * audio_rows % 16 == 0 and audio_rows % 8 == 0

time: 32.6 us -> 30.8 us (0.945)
  Pallas kernels: 29.9 us -> 28.1 us
    pallas_call x1, Pallas kernels: 29.2 us -> 27.4 us  [fused_shards(): pl.pallas_call(functools.partial(fused_kernel, n, ratio), out_shape=tuple...]
where the time goes in v2:
time: 30.8 us; the launch traced here: 30.7 us
  Pallas kernels  28.1 us (91%)
  between operations  2.58 us (8%)
    pallas_call x1, Pallas kernels, fused_shards(): pl.pallas_call(functools.partial(fused_kernel, n, ratio), out_shape=tuple...  27.4 us
    pallas_call x1, Pallas kernels, fused_shards(): pl.pallas_call(write_out, out_shape=tuple((jax.ShapeDtypeStruct(shape, jn...  0.73 us

profile of v2, /device:TPU:0, one launch (start us, length us, event | category | flops | bytes accessed | tf_op | source)
XLA Modules:
  0.0 30.7 jit_solution(11653084315866353557)
XLA Ops:
  2.6 27.4 %shard_map.174 = (bf16[16,4096]{1,0:T(8,128)(2,1)S(1)}, bf16[8,2048]{1,0:T(8,128)(2,1)S(1)}, bf16[16,2048]{1,0:T(8,128)(2,1)S(1)}, bf16[8,2048]{1,0:T(8,128)(2,1)S(1)}) custom-call(s32[1]{0:T(128)S(6)} %copy.19.refs_0_, s32[1]{0:T(128)S(6)} %copy.20.refs_1_, s32[1]{0:T(128)S(6)} %copy.21.refs_2_, bf16[16,4096]{1,0:T(8,128)(2,1)} %refs_3_.1, ...), custom_call_target="tpu_custom_call" | custom-call | tf_op jit(solution)/shard_map/pallas_call | solution.py:658
  29.9 0.7 %shard_map.175 = (bf16[16,4096]{1,0:T(8,128)(2,1)}, bf16[8,2048]{1,0:T(8,128)(2,1)}, bf16[16,2048]{1,0:T(8,128)(2,1)}, bf16[8,2048]{1,0:T(8,128)(2,1)}) custom-call(bf16[16,4096]{1,0:T(8,128)(2,1)S(1)} %get-tuple-element.8.refs_0_, bf16[8,2048]{1,0:T(8,128)(2,1)S(1)} %get-tuple-element.9.refs_1_, bf16[16,2048]{1,0:T(8,128)(2,1)S(1)} %get-tuple-element.10.refs_2_, ...), custom_call_target="tpu_custom_call" | custom-call | tf_op jit(solution)/shard_map/pallas_call | solution.py:677

commit v3 on v2

--- a/solution.py
+++ b/solution.py
@@ -279,6 +279,8 @@
 
 LANES = 128
 mark = lambda name: contextlib.nullcontext()
+KEYED = (7, 8)
+PARTIAL = 3
 
 GROUPS = (
     ((0, 1, 2), 0, False),
@@ -338,7 +340,9 @@
     outs = refs[15:19]
     held = refs[19:31]
     results = refs[31:35]
-    send_sem, far_sem, recv_sem, back_send, back_recv, stage_sem = refs[35:]
+    send_sem, far_sem, recv_sem, back_send, back_recv, stage_sem, part_sem, guest, part_out, part_in = refs[
+        35:
+    ]
     half = n // 2
     quarter = n // 4
     margin = held[7].shape[0] - half
@@ -346,6 +350,15 @@
     side = me // half
     inner = lax.rem(me, half)
     near = (me >= half - margin) & (me < half + margin)
+    lower = side == 0
+    upper = side == 1
+    hosted = near & lower
+    edge_key = near & upper
+
+    def arrival(at, same):
+        if at in KEYED and same:
+            return recv_sem.at[jnp.where(edge_key, 12 + KEYED.index(at), at)]
+        return recv_sem.at[at]
 
     def columns(width, owner):
         return pl.ds(pl.multiple_of(owner * width, LANES), width)
@@ -357,12 +370,12 @@
             return me - to_side * (half - margin)
         return me
 
-    def send(at, owner, slot, peer, sem):
+    def send(at, owner, slot, peer, sem, same):
         pltpu.make_async_remote_copy(
             src_ref=arrays[at].at[:, columns(held[at].shape[2], owner)],
             dst_ref=held[at].at[slot],
             send_sem=sem.at[at],
-            recv_sem=recv_sem.at[at],
+            recv_sem=arrival(at, same),
             device_id={"seq": peer},
             device_id_type=pl.DeviceIdType.MESH,
         ).start()
@@ -372,7 +385,7 @@
             pltpu.make_async_copy(
                 arrays[at].at[:, columns(held[at].shape[2], inner if halved else me)],
                 held[at].at[slot_of(group, which, halved, at, side)],
-                recv_sem.at[at],
+                arrival(at, True),
             ).start()
 
     col = quarter // 2
@@ -426,10 +439,10 @@
                     if halved and at == group[0] and not same:
                         continue
                     slot = slot_of(group, which, halved, at, side if same else 1 - side)
-                    send(at, owner, slot, peer, send_sem if same else far_sem)
+                    send(at, owner, slot, peer, send_sem if same else far_sem, same)
 
         if which == 3 and not same:
-            pl.when(near)(sends)
+            pl.when(hosted)(sends)
         else:
             sends()
 
@@ -437,8 +450,31 @@
         send_part(number, far_edge, quarter, 0, False)
         send_part(number, far_center, quarter, 0, False)
 
+    def k(number):
+        send_part(number, far_center, quarter, 0, False)
+
+    def g(number):
+        send_part(number, far_edge, quarter, 0, False)
+
     def s(number):
         send_part(number, sibling, quarter, 0, True)
+
+    def v(number):
+        group = GROUPS[number][0]
+
+        @pl.when(hosted)
+        def _():
+            @pl.loop(0, half)
+            def _(step):
+                owner = lax.rem(inner + step, half)
+                pltpu.make_async_remote_copy(
+                    src_ref=arrays[group[0]].at[:, columns(held[group[0]].shape[2], owner)],
+                    dst_ref=guest.at[me - (half - margin)],
+                    send_sem=far_sem.at[group[0]],
+                    recv_sem=recv_sem.at[14],
+                    device_id={"seq": half + owner},
+                    device_id_type=pl.DeviceIdType.MESH,
+                ).start()
 
     def h(number):
         send_part(number, here, quarter, 1, True)
@@ -465,13 +501,14 @@
             pl.semaphore_wait(stage_sem.at[3], 1)
         signal(stage_sem.at[4], sibling + rank)
         send_part(0, far_edge, quarter, 0, False)
+        v(3)
         f(1)
         f(3)
         f(2)
+        h(3)
+        s(3)
         h(1)
         s(1)
-        h(3)
-        s(3)
         h(2)
         s(2)
 
@@ -482,19 +519,19 @@
         send_part(0, here + mine_col, col, 1, True)
         with mark("A"):
             pl.semaphore_wait(stage_sem.at[1], 1)
+        send_part(0, far_center, quarter, 0, False)
         send_part(0, sibling + next_col, col, 0, True)
-        send_part(0, far_center, quarter, 0, False)
         with mark("C"):
             pl.semaphore_wait(stage_sem.at[4], 1)
         send_part(0, far_edge, quarter, 0, False)
         send_part(0, here + next_col, col, 0, True)
+        s(3)
         f(1)
         s(1)
-        s(3)
         f(2)
         s(2)
+        h(3)
         h(1)
-        h(3)
         h(2)
 
     video_valid = video_length[0]
@@ -525,21 +562,166 @@
             spots = lax.shift_right_logical(spots, ratio.bit_length() - 1)
             center = jnp.clip(spots + shift, 0, audio_valid - 1)
             return (where < audio_valid) & (jnp.abs(where - center) <= audio_reach)
-        where = key_places((half + margin) * video_rows) + side * (half - margin) * video_rows
-        spots = query_places(half * audio_rows, copies, side * half * audio_rows)
+        return reach_permit(copies, side * half * audio_rows, half * audio_rows, side * (half - margin) * video_rows, (half + margin) * video_rows)
+
+    def reach_permit(copies, query_first, query_count, key_first, key_count):
+        where = key_places(key_count) + key_first
+        spots = query_places(query_count, copies, query_first)
         center = jnp.clip((spots - shift) * ratio, 0, video_valid - 1)
         return (where < video_valid) & (jnp.abs(where - center) <= video_reach)
 
+    def spread(tokens):
+        lane = lax.broadcasted_iota(jnp.int32, tokens.shape, 1) // HDA
+        zero = jnp.zeros_like(tokens)
+        return jnp.concatenate(
+            [jnp.where(lane == head, tokens, zero) for head in range(LANES // HDA)], axis=0
+        )
+
+    def fold(stacked):
+        rows = stacked.shape[0] // (LANES // HDA)
+        merged = jnp.broadcast_to(stacked[:rows], (rows, LANES))
+        lane = lax.broadcasted_iota(jnp.int32, merged.shape, 1) // HDA
+        for head in range(1, LANES // HDA):
+            merged = jnp.where(lane == head, stacked[head * rows : (head + 1) * rows], merged)
+        return merged
+
+    def scored(tokens, keys, permit):
+        scores = lax.dot_general(
+            tokens, keys, (((1,), (1,)), ((), ())), preferred_element_type=jnp.float32
+        )
+        return jnp.where(permit, scores * (1.0 / math.sqrt(HDA)), -1e30)
+
+    def weighed(scores, peak, permit, values):
+        weights = jnp.where(permit, jnp.exp(scores - peak), 0.0)
+        total = jnp.sum(weights, axis=1, keepdims=True)
+        mixed = jnp.dot(weights.astype(jnp.bfloat16), values, preferred_element_type=jnp.float32)
+        return mixed, total
+
+    def tokens_of(ref, first, count, column):
+        block = ref[first : first + count, :, column : column + LANES]
+        rows = block.shape[1]
+        if rows % 16:
+            return block.astype(jnp.float32).reshape(count * rows, LANES).astype(block.dtype)
+        return block.reshape(count * rows, LANES)
+
+    group3 = GROUPS[3][0]
+    heads_each = LANES // HDA
+
+    def host_guests():
+        copies = heads_each
+        permit = reach_permit(
+            copies,
+            (half - margin) * audio_rows,
+            margin * audio_rows,
+            half * video_rows,
+            margin * video_rows,
+        )
+        with mark("WG"):
+            pltpu.make_async_copy(guest, guest, recv_sem.at[14]).wait()
+            for at in KEYED:
+                part = held[at].at[pl.ds(0, margin)]
+                pltpu.make_async_copy(part, part, recv_sem.at[12 + KEYED.index(at)]).wait()
+        keys, values = held[group3[1]], held[group3[2]]
+        rows = margin * audio_rows
+        lane = lax.broadcasted_iota(jnp.int32, (rows, LANES), 1)
+        packed = jnp.zeros((rows, LANES), jnp.float32)
+        for column in range(0, guest.shape[2], LANES):
+            tokens = spread(tokens_of(guest, 0, margin, column))
+            scores = scored(tokens, tokens_of(keys, margin, margin, column), permit)
+            peak = jnp.max(scores, axis=1, keepdims=True).astype(jnp.bfloat16).astype(jnp.float32)
+            mixed, total = weighed(scores, peak, permit, tokens_of(values, margin, margin, column))
+            coarse = total.astype(jnp.bfloat16).astype(jnp.float32)
+            for head in range(copies):
+                spot = column // LANES * copies + head
+                piece = slice(head * rows, (head + 1) * rows)
+                for kind, stat in enumerate((peak, coarse, total - coarse)):
+                    packed = jnp.where(lane == 3 * spot + kind, stat[piece], packed)
+            part_out[:, :, column : column + LANES] = (
+                fold(mixed).reshape(margin, audio_rows, LANES).astype(part_out.dtype)
+            )
+        part_out[:, :, guest.shape[2] :] = packed.reshape(margin, audio_rows, LANES).astype(
+            part_out.dtype
+        )
+        pltpu.make_async_remote_copy(
+            src_ref=part_out,
+            dst_ref=part_in,
+            send_sem=part_sem.at[0],
+            recv_sem=part_sem.at[1],
+            device_id={"seq": inner},
+            device_id_type=pl.DeviceIdType.MESH,
+        ).start()
+
+    def wait_reach():
+        for at in group3:
+            with mark("W3_%d" % at):
+                part = held[at].at[pl.ds(0, half)]
+                pltpu.make_async_copy(part, part, recv_sem.at[at]).wait()
+
+    def lower_reach():
+        copies = heads_each
+        permit = reach_permit(copies, 0, half * audio_rows, 0, half * video_rows)
+        wait_reach()
+        own = []
+        query, keys, values = (held[at] for at in group3)
+        for column in range(0, query.shape[2], LANES):
+            tokens = spread(tokens_of(query, 0, half, column))
+            scores = scored(tokens, tokens_of(keys, 0, half, column), permit)
+            peak = jnp.max(scores, axis=1, keepdims=True)
+            mixed, total = weighed(scores, peak, permit, tokens_of(values, 0, half, column))
+            own.append((fold(mixed), fold(peak), fold(total)))
+        with mark("WP"):
+            pltpu.make_async_copy(part_in, part_in, part_sem.at[1]).wait()
+        first = (half - margin) * audio_rows
+        rows = margin * audio_rows
+        stats = part_in[:, :, guest.shape[2] :].astype(jnp.float32).reshape(rows, LANES)
+        for index, (mixed, peak, total) in enumerate(own):
+            column = index * LANES
+            theirs = part_in[:, :, column : column + LANES].astype(jnp.float32).reshape(rows, LANES)
+
+            def stat(kind):
+                spots = [3 * (index * copies + head) + kind for head in range(copies)]
+                return fold(jnp.concatenate([stats[:, spot : spot + 1] for spot in spots], axis=0))
+
+            their_peak = stat(0)
+            their_total = stat(1) + stat(2)
+            top = jnp.maximum(peak[first:], their_peak)
+            mine_factor = jnp.exp(peak[first:] - top)
+            their_factor = jnp.exp(their_peak - top)
+            joined = mixed[first:] * mine_factor + theirs * their_factor
+            joined = joined / (total[first:] * mine_factor + their_total * their_factor)
+            whole = jnp.concatenate([mixed[:first] / total[:first], joined], axis=0)
+            write_tokens(results[3], column, whole)
+
+    def upper_reach():
+        copies = heads_each
+        permit = permit_of(3, copies)
+        wait_reach()
+        query, keys, values = (held[at] for at in group3)
+        for column in range(0, query.shape[2], LANES):
+            tokens = spread(read_tokens(query, column))
+            mixed = softmax_mix(
+                tokens,
+                read_tokens(keys, column),
+                read_tokens(values, column),
+                permit,
+                1.0 / math.sqrt(HDA),
+            )
+            write_tokens(results[3], column, fold(mixed))
+
     def compute(number):
         group, which, halved = GROUPS[number]
-        for at in group:
-            with mark("W%d_%d" % (which, at)):
-                pltpu.make_async_copy(held[at], held[at], recv_sem.at[at]).wait()
+        if which == 3:
+            pl.when(lower)(lower_reach)
+            pl.when(upper)(upper_reach)
+            return
         query, keys, values = (held[at] for at in group)
         depth = HDV if which == 0 else HDA
         copies = LANES // depth
         scale = 1.0 / math.sqrt(depth)
         permit = permit_of(which, copies)
+        for at in group:
+            with mark("W%d_%d" % (which, at)):
+                pltpu.make_async_copy(held[at], held[at], recv_sem.at[at]).wait()
         for column in range(0, query.shape[2], LANES):
             tokens = read_tokens(query, column)
             if copies > 1:
@@ -596,19 +778,18 @@
     compute(0)
     give_back(0, close=True)
     pl.when(central)(lambda: give_back(0, far=True))
+    pl.when(upper)(host_guests)
     compute(1)
     give_back(1, close=True)
     pl.when(central)(lambda: give_back(1, far=True))
-    compute(3)
-    give_back(3, far=False, close=True)
-    pl.when(jnp.logical_not(central))(lambda: give_back(0, far=True))
-    pl.when(jnp.logical_not(central))(lambda: give_back(1, far=True))
+    pl.when(jnp.logical_not(central) & upper)(lambda: give_back(0, far=True))
+    pl.when(jnp.logical_not(central) & upper)(lambda: give_back(1, far=True))
     compute(2)
     give_back(2, far=False, close=True)
-
-    for which in range(4):
-        with mark("R%d" % which):
-            pltpu.make_async_copy(outs[which], outs[which], back_recv.at[which]).wait()
+    compute(3)
+    pl.when(jnp.logical_not(central) & (side == 0))(lambda: give_back(0, far=True))
+    pl.when(jnp.logical_not(central) & (side == 0))(lambda: give_back(1, far=True))
+    give_back(3, far=False, close=True)
 
     def wait_bytes(ref, blocks, sem):
         part = ref.at[pl.ds(0, blocks)]
@@ -619,11 +800,19 @@
             wait_bytes(held[at], half - 1, send_sem.at[at])
             if not halved or (which == 2 and at != group[0]):
                 wait_bytes(held[at], half, far_sem.at[at])
-            elif at != group[0]:
-
-                @pl.when(near)
+            elif which == 3:
+
+                @pl.when(hosted)
                 def _(at=at):
                     wait_bytes(held[at], half, far_sem.at[at])
+
+    @pl.when(upper)
+    def _():
+        pltpu.make_async_copy(part_out, part_out, part_sem.at[0]).wait()
+
+    for which in range(4):
+        with mark("R%d" % which):
+            pltpu.make_async_copy(outs[which], outs[which], back_recv.at[which]).wait()
 
     for which in range(4):
         wait_bytes(results[which], results[which].shape[0] - 1, back_send.at[which])
@@ -645,6 +834,13 @@
     arrays = [pltpu.with_memory_space_constraint(a, pltpu.HBM) for a in arrays]
     ratio = arrays[0].shape[0] // arrays[3].shape[0]
     held = [pltpu.VMEM(s, a.dtype) for s, a in zip(held_shapes(n, arrays), arrays)]
+    guest_blocks = held[7].shape[0] - n // 2
+    guest_rows, guest_width = held[9].shape[1:]
+    guests = [
+        pltpu.VMEM((guest_blocks, guest_rows, guest_width), jnp.bfloat16),
+        pltpu.VMEM((guest_blocks, guest_rows, guest_width + LANES), jnp.bfloat16),
+        pltpu.VMEM((guest_blocks, guest_rows, guest_width + LANES), jnp.bfloat16),
+    ]
     results = [
         pltpu.VMEM((n, *held[0].shape[1:]), jnp.bfloat16),
         pltpu.VMEM((n, *held[3].shape[1:]), jnp.bfloat16),
@@ -665,10 +861,12 @@
         + [
             pltpu.SemaphoreType.DMA((12,)),
             pltpu.SemaphoreType.DMA((12,)),
-            pltpu.SemaphoreType.DMA((12,)),
+            pltpu.SemaphoreType.DMA((15,)),
             pltpu.SemaphoreType.DMA((4,)),
             pltpu.SemaphoreType.DMA((4,)),
             pltpu.SemaphoreType.REGULAR((6,)),
+            pltpu.SemaphoreType.DMA((2,)),
+            *guests,
         ],
         compiler_params=pltpu.CompilerParams(
             collective_id=0, has_side_effects=True, vmem_limit_bytes=24 * 2**20

time: 30.8 us -> 30.3 us (0.984)
  Pallas kernels: 28.1 us -> 27.5 us
    pallas_call x1, Pallas kernels: 27.4 us -> 26.8 us  [fused_shards(): pl.pallas_call(functools.partial(fused_kernel, n, ratio), out_shape=tuple...]
where the time goes in v3:
time: 30.3 us; the launch traced here: 30.1 us
  Pallas kernels  27.5 us (91%)
  between operations  2.58 us (9%)
    pallas_call x1, Pallas kernels, fused_shards(): pl.pallas_call(functools.partial(fused_kernel, n, ratio), out_shape=tuple...  26.8 us
    pallas_call x1, Pallas kernels, fused_shards(): pl.pallas_call(write_out, out_shape=tuple((jax.ShapeDtypeStruct(shape, jn...  0.73 us

profile of v3, /device:TPU:0, one launch (start us, length us, event | category | flops | bytes accessed | tf_op | source)
XLA Modules:
  0.0 30.1 jit_solution(6930184883765247715)
XLA Ops:
  2.6 26.8 %shard_map.174 = (bf16[16,4096]{1,0:T(8,128)(2,1)S(1)}, bf16[8,2048]{1,0:T(8,128)(2,1)S(1)}, bf16[16,2048]{1,0:T(8,128)(2,1)S(1)}, bf16[8,2048]{1,0:T(8,128)(2,1)S(1)}) custom-call(s32[1]{0:T(128)S(6)} %copy.19.refs_0_, s32[1]{0:T(128)S(6)} %copy.20.refs_1_, s32[1]{0:T(128)S(6)} %copy.21.refs_2_, bf16[16,4096]{1,0:T(8,128)(2,1)} %refs_3_.1, ...), custom_call_target="tpu_custom_call" | custom-call | tf_op jit(solution)/shard_map/pallas_call | solution.py:854
  29.4 0.7 %shard_map.175 = (bf16[16,4096]{1,0:T(8,128)(2,1)}, bf16[8,2048]{1,0:T(8,128)(2,1)}, bf16[16,2048]{1,0:T(8,128)(2,1)}, bf16[8,2048]{1,0:T(8,128)(2,1)}) custom-call(bf16[16,4096]{1,0:T(8,128)(2,1)S(1)} %get-tuple-element.8.refs_0_, bf16[8,2048]{1,0:T(8,128)(2,1)S(1)} %get-tuple-element.9.refs_1_, bf16[16,2048]{1,0:T(8,128)(2,1)S(1)} %get-tuple-element.10.refs_2_, ...), custom_call_target="tpu_custom_call" | custom-call | tf_op jit(solution)/shard_map/pallas_call | solution.py:875

commit v4 on v3

--- a/solution.py
+++ b/solution.py
@@ -481,7 +481,7 @@
 
     across = rank + next_col - mine_col
 
-    @pl.when(central)
+    @pl.when(central & lower)
     def _():
         signal(stage_sem.at[0], here + across)
         send_part(0, far_center + mine_col, col, 0, False)
@@ -500,11 +500,45 @@
         with mark("B"):
             pl.semaphore_wait(stage_sem.at[3], 1)
         signal(stage_sem.at[4], sibling + rank)
-        send_part(0, far_edge, quarter, 0, False)
+        g(0)
         v(3)
-        f(1)
-        f(3)
-        f(2)
+        g(1)
+        k(1)
+        g(3)
+        k(3)
+        g(2)
+        k(2)
+        h(3)
+        s(3)
+        h(1)
+        s(1)
+        h(2)
+        s(2)
+
+    @pl.when(central & upper)
+    def _():
+        signal(stage_sem.at[0], here + across)
+        send_part(0, far_center + mine_col, col, 0, False)
+        h(0)
+        with mark("Y"):
+            pl.semaphore_wait(stage_sem.at[0], 1)
+        send_part(0, far_center + next_col, col, 0, False)
+        with mark("O"):
+            pl.semaphore_wait(stage_sem.at[2], 1)
+        signal(stage_sem.at[1], sibling + rank)
+        signal(stage_sem.at[5], here + across)
+        with mark("Y2"):
+            pl.semaphore_wait(stage_sem.at[5], 1)
+        signal(stage_sem.at[3], far_center + rank)
+        s(0)
+        with mark("B"):
+            pl.semaphore_wait(stage_sem.at[3], 1)
+        signal(stage_sem.at[4], sibling + rank)
+        g(0)
+        g(1)
+        k(1)
+        g(2)
+        k(2)
         h(3)
         s(3)
         h(1)
@@ -519,16 +553,18 @@
         send_part(0, here + mine_col, col, 1, True)
         with mark("A"):
             pl.semaphore_wait(stage_sem.at[1], 1)
-        send_part(0, far_center, quarter, 0, False)
+        k(0)
         send_part(0, sibling + next_col, col, 0, True)
         with mark("C"):
             pl.semaphore_wait(stage_sem.at[4], 1)
-        send_part(0, far_edge, quarter, 0, False)
+        g(0)
         send_part(0, here + next_col, col, 0, True)
         s(3)
-        f(1)
+        g(1)
+        k(1)
         s(1)
-        f(2)
+        g(2)
+        k(2)
         s(2)
         h(3)
         h(1)
@@ -708,11 +744,10 @@
             )
             write_tokens(results[3], column, fold(mixed))
 
-    def compute(number):
+    def compute(number, low=None):
         group, which, halved = GROUPS[number]
         if which == 3:
-            pl.when(lower)(lower_reach)
-            pl.when(upper)(upper_reach)
+            (lower_reach if low else upper_reach)()
             return
         query, keys, values = (held[at] for at in group)
         depth = HDV if which == 0 else HDA
@@ -742,6 +777,9 @@
                 mixed = merged
             write_tokens(results[which], column, mixed)
 
+    def far_range(far):
+        return {1: (0, half), 2: (0, col), 3: (col, half)}[int(far)]
+
     def give_back(number, far=False, close=False):
         group, which, halved = GROUPS[number]
         mine = inner if halved else me
@@ -759,7 +797,7 @@
 
         if far:
 
-            @pl.loop(0, half)
+            @pl.loop(*far_range(far))
             def _(step):
                 peer = (1 - side) * half + step
                 give(peer, peer)
@@ -775,21 +813,41 @@
 
         pltpu.make_async_copy(results[which].at[mine], target, back_recv.at[which]).start()
 
-    compute(0)
-    give_back(0, close=True)
-    pl.when(central)(lambda: give_back(0, far=True))
-    pl.when(upper)(host_guests)
-    compute(1)
-    give_back(1, close=True)
-    pl.when(central)(lambda: give_back(1, far=True))
-    pl.when(jnp.logical_not(central) & upper)(lambda: give_back(0, far=True))
-    pl.when(jnp.logical_not(central) & upper)(lambda: give_back(1, far=True))
-    compute(2)
-    give_back(2, far=False, close=True)
-    compute(3)
-    pl.when(jnp.logical_not(central) & (side == 0))(lambda: give_back(0, far=True))
-    pl.when(jnp.logical_not(central) & (side == 0))(lambda: give_back(1, far=True))
-    give_back(3, far=False, close=True)
+    @pl.when(lower)
+    def _():
+        compute(0)
+        give_back(0, close=True)
+        pl.when(central)(lambda: give_back(0, far=1))
+        compute(1)
+        give_back(1, close=True)
+        pl.when(central)(lambda: give_back(1, far=1))
+        compute(2)
+        give_back(2, far=False, close=True)
+        compute(3, True)
+        pl.when(jnp.logical_not(central))(lambda: give_back(0, far=1))
+        pl.when(jnp.logical_not(central))(lambda: give_back(1, far=1))
+        give_back(3, far=False, close=True)
+
+    @pl.when(upper)
+    def _():
+        compute(0)
+        give_back(0, close=True)
+        pl.when(central)(lambda: give_back(0, far=2))
+        pl.when(central)(lambda: give_back(0, far=3))
+        host_guests()
+        compute(1)
+        give_back(1, close=True)
+        pl.when(central)(lambda: give_back(1, far=2))
+        pl.when(central)(lambda: give_back(1, far=3))
+        pl.when(jnp.logical_not(central))(lambda: give_back(0, far=2))
+        pl.when(jnp.logical_not(central))(lambda: give_back(1, far=2))
+        pl.when(jnp.logical_not(central))(lambda: give_back(0, far=3))
+        pl.when(jnp.logical_not(central))(lambda: give_back(1, far=3))
+        compute(2)
+        give_back(2, far=False, close=True)
+        compute(3, False)
+        give_back(3, far=False, close=True)
+
 
     def wait_bytes(ref, blocks, sem):
         part = ref.at[pl.ds(0, blocks)]

time: 30.3 us -> 29.7 us (0.980)
  Pallas kernels: 27.5 us -> 27 us
    pallas_call x1, Pallas kernels: 26.8 us -> 26.2 us  [fused_shards(): pl.pallas_call(functools.partial(fused_kernel, n, ratio), out_shape=tuple...]
where the time goes in v4:
time: 29.7 us; the launch traced here: 29.5 us
  Pallas kernels  27 us (91%)
  between operations  2.58 us (9%)
    pallas_call x1, Pallas kernels, fused_shards(): pl.pallas_call(functools.partial(fused_kernel, n, ratio), out_shape=tuple...  26.2 us
    pallas_call x1, Pallas kernels, fused_shards(): pl.pallas_call(write_out, out_shape=tuple((jax.ShapeDtypeStruct(shape, jn...  0.73 us

profile of v4, /device:TPU:0, one launch (start us, length us, event | category | flops | bytes accessed | tf_op | source)
XLA Modules:
  0.0 29.5 jit_solution(9023645741111433188)
XLA Ops:
  2.6 26.2 %shard_map.174 = (bf16[16,4096]{1,0:T(8,128)(2,1)S(1)}, bf16[8,2048]{1,0:T(8,128)(2,1)S(1)}, bf16[16,2048]{1,0:T(8,128)(2,1)S(1)}, bf16[8,2048]{1,0:T(8,128)(2,1)S(1)}) custom-call(s32[1]{0:T(128)S(6)} %copy.19.refs_0_, s32[1]{0:T(128)S(6)} %copy.20.refs_1_, s32[1]{0:T(128)S(6)} %copy.21.refs_2_, bf16[16,4096]{1,0:T(8,128)(2,1)} %refs_3_.1, ...), custom_call_target="tpu_custom_call" | custom-call | tf_op jit(solution)/shard_map/pallas_call | solution.py:912
  28.8 0.7 %shard_map.175 = (bf16[16,4096]{1,0:T(8,128)(2,1)}, bf16[8,2048]{1,0:T(8,128)(2,1)}, bf16[16,2048]{1,0:T(8,128)(2,1)}, bf16[8,2048]{1,0:T(8,128)(2,1)}) custom-call(bf16[16,4096]{1,0:T(8,128)(2,1)S(1)} %get-tuple-element.8.refs_0_, bf16[8,2048]{1,0:T(8,128)(2,1)S(1)} %get-tuple-element.9.refs_1_, bf16[16,2048]{1,0:T(8,128)(2,1)S(1)} %get-tuple-element.10.refs_2_, ...), custom_call_target="tpu_custom_call" | custom-call | tf_op jit(solution)/shard_map/pallas_call | solution.py:933

commit v5 on v4

--- a/solution.py
+++ b/solution.py
@@ -508,9 +508,9 @@
         k(3)
         g(2)
         k(2)
+        h(1)
         h(3)
         s(3)
-        h(1)
         s(1)
         h(2)
         s(2)
@@ -536,17 +536,17 @@
         signal(stage_sem.at[4], sibling + rank)
         g(0)
         g(1)
+        h(1)
         k(1)
         g(2)
         k(2)
         h(3)
         s(3)
-        h(1)
         s(1)
         h(2)
         s(2)
 
-    @pl.when(jnp.logical_not(central))
+    @pl.when(jnp.logical_not(central) & lower)
     def _():
         signal(stage_sem.at[2], sibling + rank)
         send_part(0, sibling + mine_col, col, 0, True)
@@ -563,10 +563,34 @@
         g(1)
         k(1)
         s(1)
+        k(2)
         g(2)
-        k(2)
         s(2)
         h(3)
+        h(1)
+        h(2)
+
+    @pl.when(jnp.logical_not(central) & upper)
+    def _():
+        send_part(0, here + mine_col, col, 1, True)
+        signal(stage_sem.at[2], sibling + rank)
+        send_part(0, sibling + mine_col, col, 0, True)
+        with mark("A"):
+            pl.semaphore_wait(stage_sem.at[1], 1)
+        k(0)
+        send_part(0, sibling + next_col, col, 0, True)
+        with mark("C"):
+            pl.semaphore_wait(stage_sem.at[4], 1)
+        g(0)
+        send_part(0, here + next_col, col, 0, True)
+        s(3)
+        g(1)
+        k(1)
+        s(1)
+        g(2)
+        s(2)
+        h(3)
+        k(2)
         h(1)
         h(2)
 
@@ -697,14 +721,18 @@
         copies = heads_each
         permit = reach_permit(copies, 0, half * audio_rows, 0, half * video_rows)
         wait_reach()
+        query, keys, values = (held[at] for at in group3)
         own = []
-        query, keys, values = (held[at] for at in group3)
         for column in range(0, query.shape[2], LANES):
             tokens = spread(tokens_of(query, 0, half, column))
             scores = scored(tokens, tokens_of(keys, 0, half, column), permit)
             peak = jnp.max(scores, axis=1, keepdims=True)
             mixed, total = weighed(scores, peak, permit, tokens_of(values, 0, half, column))
             own.append((fold(mixed), fold(peak), fold(total)))
+        return own
+
+    def lower_join(own):
+        copies = heads_each
         with mark("WP"):
             pltpu.make_async_copy(part_in, part_in, part_sem.at[1]).wait()
         first = (half - margin) * audio_rows
@@ -747,7 +775,7 @@
     def compute(number, low=None):
         group, which, halved = GROUPS[number]
         if which == 3:
-            (lower_reach if low else upper_reach)()
+            lower_join(lower_reach()) if low else upper_reach()
             return
         query, keys, values = (held[at] for at in group)
         depth = HDV if which == 0 else HDA
@@ -807,7 +835,7 @@
 
         @pl.loop(1, half)
         def _(step):
-            block = lax.rem(inner + step, half)
+            block = jnp.where(step <= inner, step - 1, step)
             peer = side * half + block
             give(block if halved else peer, peer)
 
@@ -816,24 +844,25 @@
     @pl.when(lower)
     def _():
         compute(0)
+        own = lower_reach()
         give_back(0, close=True)
-        pl.when(central)(lambda: give_back(0, far=1))
         compute(1)
         give_back(1, close=True)
+        pl.when(central)(lambda: give_back(0, far=1))
         pl.when(central)(lambda: give_back(1, far=1))
         compute(2)
         give_back(2, far=False, close=True)
-        compute(3, True)
         pl.when(jnp.logical_not(central))(lambda: give_back(0, far=1))
+        lower_join(own)
+        give_back(3, far=False, close=True)
         pl.when(jnp.logical_not(central))(lambda: give_back(1, far=1))
-        give_back(3, far=False, close=True)
 
     @pl.when(upper)
     def _():
         compute(0)
         give_back(0, close=True)
+        pl.when(central)(lambda: give_back(0, far=3))
         pl.when(central)(lambda: give_back(0, far=2))
-        pl.when(central)(lambda: give_back(0, far=3))
         host_guests()
         compute(1)
         give_back(1, close=True)
@@ -843,10 +872,10 @@
         pl.when(jnp.logical_not(central))(lambda: give_back(1, far=2))
         pl.when(jnp.logical_not(central))(lambda: give_back(0, far=3))
         pl.when(jnp.logical_not(central))(lambda: give_back(1, far=3))
+        compute(3, False)
+        give_back(3, far=False, close=True)
         compute(2)
         give_back(2, far=False, close=True)
-        compute(3, False)
-        give_back(3, far=False, close=True)
 
 
     def wait_bytes(ref, blocks, sem):
@@ -868,12 +897,13 @@
     def _():
         pltpu.make_async_copy(part_out, part_out, part_sem.at[0]).wait()
 
+
+    for which in range(4):
+        wait_bytes(results[which], results[which].shape[0] - 1, back_send.at[which])
+
     for which in range(4):
         with mark("R%d" % which):
             pltpu.make_async_copy(outs[which], outs[which], back_recv.at[which]).wait()
-
-    for which in range(4):
-        wait_bytes(results[which], results[which].shape[0] - 1, back_send.at[which])
 
 
 def write_out(*refs):

time: 29.7 us -> 29.6 us (level)
  no operation moved by 1% of the time
where the time goes in v5:
time: 29.6 us; the launch traced here: 29.4 us
  Pallas kernels  26.8 us (91%)
  between operations  2.58 us (9%)
    pallas_call x1, Pallas kernels, fused_shards(): pl.pallas_call(functools.partial(fused_kernel, n, ratio), out_shape=tuple...  26.1 us
    pallas_call x1, Pallas kernels, fused_shards(): pl.pallas_call(write_out, out_shape=tuple((jax.ShapeDtypeStruct(shape, jn...  0.73 us

profile of v5, /device:TPU:0, one launch (start us, length us, event | category | flops | bytes accessed | tf_op | source)
XLA Modules:
  0.0 29.4 jit_solution(14646334031427033402)
XLA Ops:
  2.6 26.1 %shard_map.174 = (bf16[16,4096]{1,0:T(8,128)(2,1)S(1)}, bf16[8,2048]{1,0:T(8,128)(2,1)S(1)}, bf16[16,2048]{1,0:T(8,128)(2,1)S(1)}, bf16[8,2048]{1,0:T(8,128)(2,1)S(1)}) custom-call(s32[1]{0:T(128)S(6)} %copy.19.refs_0_, s32[1]{0:T(128)S(6)} %copy.20.refs_1_, s32[1]{0:T(128)S(6)} %copy.21.refs_2_, bf16[16,4096]{1,0:T(8,128)(2,1)} %refs_3_.1, ...), custom_call_target="tpu_custom_call" | custom-call | tf_op jit(solution)/shard_map/pallas_call | solution.py:942
  28.7 0.7 %shard_map.175 = (bf16[16,4096]{1,0:T(8,128)(2,1)}, bf16[8,2048]{1,0:T(8,128)(2,1)}, bf16[16,2048]{1,0:T(8,128)(2,1)}, bf16[8,2048]{1,0:T(8,128)(2,1)}) custom-call(bf16[16,4096]{1,0:T(8,128)(2,1)S(1)} %get-tuple-element.8.refs_0_, bf16[8,2048]{1,0:T(8,128)(2,1)S(1)} %get-tuple-element.9.refs_1_, bf16[16,2048]{1,0:T(8,128)(2,1)S(1)} %get-tuple-element.10.refs_2_, ...), custom_call_target="tpu_custom_call" | custom-call | tf_op jit(solution)/shard_map/pallas_call | solution.py:963
